TPU v7x, 32 devices: a whole 2x2x4 slice. The times are simulated.
32 devices in a mesh: groups: 2 (over x), blk: 16 (over z, y, core).
Axes of the slice: x: 2, y: 2, z: 4, core: 2. Of those that a mesh axis runs over, the one named last changes fastest.
Arguments:
- queries: bfloat16 [24576, 1536], P(('groups', 'blk')), parts along dimension 0, may hold values from -20 to 20
- keys: bfloat16 [24576, 1536], P(('groups', 'blk')), parts along dimension 0, may hold values from -6 to 6
- values: bfloat16 [24576, 1536], P(('groups', 'blk')), parts along dimension 0, may hold values from -6 to 6
- neighbours: int32 [64, 7], P(('groups', 'blk')), parts along dimension 0, may hold values from -1 to 31, as said below
Outputs:
- attended: bfloat16 [24576, 1536], P(('groups', 'blk')), parts along dimension 0
There are 2 independent parts, one for each index of `groups`. A program takes and returns all parts, laid end to end along the dimension named above; each array names one. Nothing has to cross between parts.
Inputs may be any that keep to these rules, and one draw needn't show every extreme that they name: `neighbours`: entry 0 of row t is t itself. Every other non-negative entry names a distinct tile of a frame block at most two blocks away from tile t's block; a slot is -1 only where its drawn tile falls outside the clip.
All inputs are finite; a program needn't handle non-finite values.
Results may differ from a plain program's by a relative error of at most 0.0048.
Values may be sent and summed in bfloat16 or wider, within the bound.
A program may use at most 128 MiB of HBM per device.

v0:
```python
import functools
import math

import jax
import jax.numpy as jnp
from jax import lax
from jax.experimental import pallas as pl
from jax.experimental.pallas import tpu as pltpu
from jax.sharding import PartitionSpec as P

HD = 128
WINDOW = 5
ROWS = 384


def kernel(count, heads, named, queries, keys, values, out, *scratch):
    windows = (scratch[:heads], scratch[heads : 2 * heads])
    (held_q, held_o, local_sem, q_sem, o_sem, y_send, y_recv, sib_send, sib_recv,
     z_send, z_recv, share_send, share_recv) = scratch[2 * heads :]
    sources = (keys, values)
    tiles, tile_len, _ = queries.shape
    slots = named.shape[1]
    rows = min(ROWS, tile_len)
    factor = math.log2(math.e) * HD ** -0.5

    me = lax.axis_index("blk")
    core = lax.rem(me, 2)
    side = lax.rem(me // 2, 2)
    quad = me // 4
    last = count // 4 - 1
    sibling = me + 1 - 2 * core
    partner = me + 2 - 4 * side
    ahead = me + 4 - 8 * side
    can_relay = jnp.where(side == 0, quad < last, quad > 0)
    gets_relay = jnp.where(side == 0, quad > 0, quad < last)
    shares_partner = core == side
    partner_at = 4 - 4 * side
    relay_at = 4 * side

    def part(ref, block):
        return ref.at[pl.ds(block * tiles, tiles)]

    def columns(ref, head):
        return ref.at[:, :, pl.ds(head * HD, HD)]

    def local_copy(head, which):
        return pltpu.make_async_copy(
            columns(sources[which], head), part(windows[which][head], 2), local_sem.at[head, which]
        )

    def remote(src, dst, send, recv, head, which, target):
        return pltpu.make_async_remote_copy(
            src_ref=src, dst_ref=dst, send_sem=send.at[head, which], recv_sem=recv.at[head, which],
            device_id={"blk": target}, device_id_type=pl.DeviceIdType.MESH,
        )

    def partner_copy(head, which):
        return remote(columns(sources[which], head), part(windows[which][head], relay_at),
                      y_send, y_recv, head, which, partner)

    def sibling_copy(head, which):
        return remote(columns(sources[which], head), part(windows[which][head], 1 + 2 * core),
                      sib_send, sib_recv, head, which, sibling)

    def relay_copy(head, which):
        window = windows[which][head]
        return remote(part(window, partner_at), part(window, relay_at),
                      z_send, z_recv, head, which, ahead)

    def share_copy(head, which):
        window = windows[which][head]
        return remote(part(window, 4 - 4 * core), part(window, 3 - 2 * core),
                      share_send, share_recv, head, which, sibling)

    def query_copy(head):
        return pltpu.make_async_copy(columns(queries, head), columns(held_q, head), q_sem.at[head])

    def out_copy(head):
        return pltpu.make_async_copy(columns(held_o, head), columns(out, head), o_sem.at[head])

    barrier = pltpu.get_barrier_semaphore()

    def greet(target):
        pl.semaphore_signal(barrier, inc=1, device_id={"blk": target}, device_id_type=pl.DeviceIdType.MESH)

    greet(sibling)
    greet(partner)

    @pl.when(quad > 0)
    def _():
        greet(me - 4)

    @pl.when(quad < last)
    def _():
        greet(me + 4)

    pl.semaphore_wait(barrier, 2 + (quad > 0).astype(jnp.int32) + (quad < last).astype(jnp.int32))

    for head in range(heads):
        for which in range(2):
            partner_copy(head, which).start()
        for which in range(2):
            sibling_copy(head, which).start()
            local_copy(head, which).start()
        query_copy(head).start()

    def attend(head):
        key_window, value_window = windows[0][head], windows[1][head]
        start = head * HD
        per_tile = tile_len // rows

        def block(index, carry):
            tile = index // per_tile
            row = pl.multiple_of(lax.rem(index, per_tile) * rows, rows)
            query = held_q[tile, pl.ds(row, rows), start : start + HD]
            own = 2 * tiles + tile
            base = (me - 2) * tiles
            scores, peaks, valid, places = [], [], [], []
            for slot in range(slots):
                entry = named[tile, slot]
                ok = entry >= 0
                place = jnp.clip(jnp.where(ok, entry - base, own), 0, WINDOW * tiles - 1)
                score = lax.dot_general(
                    query, key_window[place], (((1,), (1,)), ((), ())),
                    preferred_element_type=jnp.float32,
                )
                peak = jnp.max(score, axis=1, keepdims=True)
                peaks.append(jnp.where(ok, peak, -jnp.inf))
                scores.append(score)
                valid.append(ok)
                places.append(place)
            top = functools.reduce(jnp.maximum, peaks) * factor
            total = jnp.zeros((rows, 1), jnp.float32)
            summed = jnp.zeros((rows, HD), jnp.float32)
            for slot in range(slots):
                offset = jnp.where(valid[slot], top, jnp.inf)
                weights = jnp.exp2(scores[slot] * factor - offset)
                total += jnp.sum(weights, axis=1, keepdims=True)
                summed += jnp.dot(
                    weights.astype(jnp.bfloat16), value_window[places[slot]],
                    preferred_element_type=jnp.float32,
                )
            held_o[tile, pl.ds(row, rows), start : start + HD] = (summed / total).astype(held_o.dtype)
            return carry

        lax.fori_loop(0, tiles * per_tile, block, 0)

    for step in range(heads + 1):
        if step < heads:
            for which in range(2):
                partner_copy(step, which).wait_recv()

                @pl.when(can_relay)
                def _():
                    relay_copy(step, which).start()

                @pl.when(shares_partner)
                def _():
                    share_copy(step, which).start()

        if step > 0:
            head = step - 1
            for which in range(2):

                @pl.when(gets_relay)
                def _():
                    relay_copy(head, which).wait_recv()

                    @pl.when(jnp.logical_not(shares_partner))
                    def _():
                        share_copy(head, which).start()

            query_copy(head).wait()
            for which in range(2):
                local_copy(head, which).wait()
                sibling_copy(head, which).wait_recv()

                @pl.when(jnp.logical_or(jnp.logical_not(shares_partner), gets_relay))
                def _():
                    share_copy(head, which).wait_recv()

            attend(head)
            out_copy(head).start()

    for head in range(heads):
        out_copy(head).wait()
        for which in range(2):
            partner_copy(head, which).wait_send()
            sibling_copy(head, which).wait_send()

            @pl.when(can_relay)
            def _():
                relay_copy(head, which).wait_send()

            @pl.when(jnp.logical_or(shares_partner, gets_relay))
            def _():
                share_copy(head, which).wait_send()


def on_device(count, queries, keys, values, neighbours):
    tokens, width = queries.shape
    tiles = neighbours.shape[0]
    tile_len = tokens // tiles
    heads = width // HD
    shape = (tiles, tile_len, width)
    window = pltpu.VMEM((WINDOW * tiles, tile_len, HD), queries.dtype)
    pair = pltpu.SemaphoreType.DMA((heads, 2))
    single = pltpu.SemaphoreType.DMA((heads,))
    hbm = pl.BlockSpec(memory_space=pl.ANY)
    out = pl.pallas_call(
        functools.partial(kernel, count, heads),
        out_shape=jax.ShapeDtypeStruct(shape, queries.dtype),
        in_specs=[pl.BlockSpec(memory_space=pltpu.SMEM), hbm, hbm, hbm],
        out_specs=hbm,
        scratch_shapes=[window] * (2 * heads)
        + [pltpu.VMEM(shape, queries.dtype)] * 2
        + [pair, single, single]
        + [pair] * 8,
        compiler_params=pltpu.CompilerParams(
            collective_id=0, has_side_effects=True, vmem_limit_bytes=60 * 1024 * 1024
        ),
    )(neighbours, queries.reshape(shape), keys.reshape(shape), values.reshape(shape))
    return out.reshape(tokens, width)


def solution(mesh):
    spec = P(("groups", "blk"), None)
    return jax.shard_map(
        functools.partial(on_device, mesh.shape["blk"]),
        mesh=mesh, in_specs=(spec,) * 4, out_specs=spec, check_vma=False,
    )
```

profile of v0, /device:TPU:15, one launch (start us, length us, event | category | flops | bytes accessed | tf_op | source)
XLA Modules:
  0.0 123.9 jit_solution(15374692411765399938)
XLA Ops:
  0.0 120.6 %shard_map.46 = bf16[2,384,1536]{2,1,0:T(8,128)(2,1)} custom-call(s32[2,7]{1,0:T(2,128)} %named.1, bf16[2,384,1536]{2,1,0:T(8,128)(2,1)} %bitcast.5, bf16[2,384,1536]{2,1,0:T(8,128)(2,1)} %bitcast.6, bf16[2,384,1536]{2,1,0:T(8,128)(2,1)} %bitcast.7), custom_call_target="tpu_custom_call" | custom-call | tf_op jit(solution)/shard_map/pallas_call | solution.py:210
  120.6 3.2 %copy.6 = bf16[768,1536]{1,0:T(8,128)(2,1)} copy(bf16[768,1536]{1,0:T(8,128)(2,1)} %bitcast.4) | data formatting | bytes 4718592
where the time goes:
time: 124 us
  Pallas kernels  121 us (98%)
  local copies, waits for them, and re-layouts  3.22 us (3%)
    pallas_call x1, Pallas kernels, on_device(): pl.pallas_call(functools.partial(kernel, count, heads), out_shape=jax.Sha...  121 us
    unnamed x1, local copies, waits for them, and re-layouts  3.22 us

commit v1 on v0

v1 whole, which is shorter than its diff:
```python
import functools
import math

import jax
import jax.numpy as jnp
from jax import lax
from jax.experimental import pallas as pl
from jax.experimental.pallas import tpu as pltpu
from jax.sharding import PartitionSpec as P

HD = 128
WINDOW = 5
PIECES = 4


def kernel(count, heads, named, queries, keys, values, out, *scratch):
    windows = (scratch[:heads], scratch[heads : 2 * heads])
    (scores, tops, held_q, held_o, local_sem, q_sem, o_sem, y_send, y_recv, sib_send, sib_recv,
     z_send, z_recv, share_send, share_recv) = scratch[2 * heads :]
    sources = (keys, values)
    tiles, tile_len, _ = queries.shape
    slots = named.shape[1]
    rows = tile_len // PIECES
    per_tile = PIECES // tiles
    factor = math.log2(math.e) * HD ** -0.5

    me = lax.axis_index("blk")
    core = lax.rem(me, 2)
    side = lax.rem(me // 2, 2)
    quad = me // 4
    last = count // 4 - 1
    sibling = me + 1 - 2 * core
    partner = me + 2 - 4 * side
    ahead = me + 4 - 8 * side
    behind = me - 4 + 8 * side
    can_relay = jnp.where(side == 0, quad < last, quad > 0)
    gets_relay = jnp.where(side == 0, quad > 0, quad < last)
    shares_partner = core == side
    shares_relay = jnp.logical_and(jnp.logical_not(shares_partner), gets_relay)
    partner_at = 4 - 4 * side
    relay_at = 4 * side

    def strip(head):
        return pl.ds(head * HD, HD)

    def part(ref, block, piece=None):
        at = pl.ds(block * tiles, tiles)
        return ref.at[at] if piece is None else ref.at[at, pl.ds(piece * rows, rows)]

    def remote(src, dst, send, recv, target):
        return pltpu.make_async_remote_copy(
            src_ref=src, dst_ref=dst, send_sem=send, recv_sem=recv,
            device_id={"blk": target}, device_id_type=pl.DeviceIdType.MESH,
        )

    def partner_copy(head, which, piece=None):
        window = windows[which][head]
        if piece is None:
            src = sources[which].at[:, :, strip(head)]
        else:
            src = sources[which].at[:, pl.ds(piece * rows, rows), strip(head)]
        recv = y_recv.at[head, which, 0 if piece is None else piece]
        return remote(src, part(window, relay_at, piece), y_send.at[head, which], recv, partner)

    def relay_copy(head, which, piece=None):
        window = windows[which][head]
        recv = z_recv.at[head, which, 0 if piece is None else piece]
        return remote(part(window, partner_at, piece), part(window, relay_at, piece),
                      z_send.at[head, which], recv, ahead)

    def share_copy(head, which, piece=None):
        window = windows[which][head]
        return remote(part(window, 4 - 4 * core, piece), part(window, 3 - 2 * core, piece),
                      share_send.at[head, which], share_recv.at[head, which], sibling)

    def sibling_copy(head, which, tile=None):
        window, source = windows[which][head], sources[which]
        at = (1 + 2 * core) * tiles
        if tile is None:
            src, dst = source.at[:, :, strip(head)], window.at[pl.ds(at, tiles)]
        else:
            src, dst = source.at[tile, :, strip(head)], window.at[at + tile]
        return remote(src, dst, sib_send.at[head, which], sib_recv.at[head, which], sibling)

    def local_copy(head, which, tile=None):
        window, source = windows[which][head], sources[which]
        if tile is None:
            src, dst = source.at[:, :, strip(head)], part(window, 2)
        else:
            src, dst = source.at[tile, :, strip(head)], window.at[2 * tiles + tile]
        return pltpu.make_async_copy(src, dst, local_sem.at[head, which])

    def query_copy(head, tile=None):
        if tile is None:
            return pltpu.make_async_copy(queries.at[:, :, strip(head)], held_q.at[:, :, strip(head)], q_sem.at[head])
        return pltpu.make_async_copy(
            queries.at[tile, :, strip(head)], held_q.at[tile, :, strip(head)], q_sem.at[head])

    def out_copy(head, tile=None):
        if tile is None:
            return pltpu.make_async_copy(held_o.at[:, :, strip(head)], out.at[:, :, strip(head)], o_sem.at[head])
        return pltpu.make_async_copy(
            held_o.at[tile, :, strip(head)], out.at[tile, :, strip(head)], o_sem.at[head])

    def send(head, which, tile):
        for j in range(per_tile):
            partner_copy(head, which, tile * per_tile + j).start()
        sibling_copy(head, which, tile).start()
        local_copy(head, which, tile).start()
        if which == 0:
            query_copy(head, tile).start()

    def pass_on(head, which, piece):
        partner_copy(head, which, piece).wait_recv()

        @pl.when(can_relay)
        def _():
            relay_copy(head, which, piece).start()

        @pl.when(shares_partner)
        def _():
            share_copy(head, which, piece).start()

    def share_relay(head, which, piece):
        @pl.when(shares_relay)
        def _():
            relay_copy(head, which, piece).wait_recv()
            share_copy(head, which, piece).start()

    def gather(head, which):
        local_copy(head, which).wait()
        sibling_copy(head, which).wait_recv()

        @pl.when(jnp.logical_and(shares_partner, gets_relay))
        def _():
            for piece in range(PIECES):
                relay_copy(head, which, piece).wait_recv()

        @pl.when(jnp.logical_or(jnp.logical_not(shares_partner), gets_relay))
        def _():
            share_copy(head, which).wait_recv()

    def drain(head):
        for which in range(2):
            partner_copy(head, which).wait_send()
            sibling_copy(head, which).wait_send()

            @pl.when(can_relay)
            def _():
                relay_copy(head, which).wait_send()

            @pl.when(jnp.logical_or(shares_partner, gets_relay))
            def _():
                share_copy(head, which).wait_send()

    def place_of(tile, slot):
        entry = named[tile, slot]
        ok = entry >= 0
        place = jnp.where(ok, entry - (me - 2) * tiles, 2 * tiles + tile)
        return ok, jnp.clip(place, 0, WINDOW * tiles - 1)

    def score(head, tile):
        query = held_q[tile, :, strip(head)]
        peaks = []
        for slot in range(slots):
            ok, place = place_of(tile, slot)
            score = lax.dot_general(
                query, windows[0][head][place], (((1,), (1,)), ((), ())),
                preferred_element_type=jnp.float32,
            )
            scores[tile, slot] = score
            peaks.append(jnp.where(ok, jnp.max(score, axis=1, keepdims=True), -jnp.inf))
        tops[tile] = jnp.broadcast_to(functools.reduce(jnp.maximum, peaks) * factor, tops.shape[1:])

    def mix(head, tile):
        total = jnp.zeros((tile_len, 1), jnp.float32)
        summed = jnp.zeros((tile_len, HD), jnp.float32)
        top = tops[tile, :, 0:1]
        for slot in range(slots):
            ok, place = place_of(tile, slot)
            offset = jnp.where(ok, top, jnp.inf)
            weights = jnp.exp2(scores[tile, slot] * factor - offset)
            total += jnp.sum(weights, axis=1, keepdims=True)
            summed += jnp.dot(
                weights.astype(jnp.bfloat16), windows[1][head][place],
                preferred_element_type=jnp.float32,
            )
        held_o[tile, :, strip(head)] = (summed / total).astype(held_o.dtype)

    barrier = pltpu.get_barrier_semaphore()

    def greet(target):
        pl.semaphore_signal(barrier, inc=1, device_id={"blk": target}, device_id_type=pl.DeviceIdType.MESH)

    greet(partner)
    greet(sibling)

    @pl.when(gets_relay)
    def _():
        greet(behind)

    pl.semaphore_wait(barrier, 2 + can_relay.astype(jnp.int32))

    for which in range(2):
        for tile in range(tiles):
            send(0, which, tile)

    for step in range(heads + 1):
        head = step - 1
        for which in range(2):
            if step == heads:
                for piece in range(PIECES):
                    if which == 0:
                        share_relay(head, 1, piece)

            @pl.loop(0, tiles)
            def _(tile):
                for j in range(per_tile):
                    piece = tile * per_tile + j
                    if step < heads:
                        pass_on(step, which, piece)
                        if which == 1:
                            share_relay(step, 0, piece)
                        elif head >= 0:
                            share_relay(head, 1, piece)
                    if j == 0:
                        if step + 1 < heads:
                            send(step + 1, which, tile)
                        if head > 0 and which == 0:
                            @pl.when(tile == tiles - 1)
                            def _():
                                drain(head - 1)
                if head >= 0:
                    @pl.when(tile == 0)
                    def _():
                        if which == 0:
                            query_copy(head).wait()
                        gather(head, which)

                    if which == 0:
                        score(head, tile)
                    else:
                        mix(head, tile)
                        out_copy(head, tile).start()

    drain(heads - 1)
    for head in range(heads):
        out_copy(head).wait()


def on_device(count, queries, keys, values, neighbours):
    tokens, width = queries.shape
    tiles, slots = neighbours.shape
    tile_len = tokens // tiles
    heads = width // HD
    shape = (tiles, tile_len, width)
    window = pltpu.VMEM((WINDOW * tiles, tile_len, HD), queries.dtype)
    single = pltpu.SemaphoreType.DMA((heads,))
    pair = pltpu.SemaphoreType.DMA((heads, 2))
    each = pltpu.SemaphoreType.DMA((heads, 2, PIECES))
    hbm = pl.BlockSpec(memory_space=pl.ANY)
    out = pl.pallas_call(
        functools.partial(kernel, count, heads),
        out_shape=jax.ShapeDtypeStruct(shape, queries.dtype),
        in_specs=[pl.BlockSpec(memory_space=pltpu.SMEM), hbm, hbm, hbm],
        out_specs=hbm,
        scratch_shapes=[window] * (2 * heads)
        + [pltpu.VMEM((tiles, slots, tile_len, tile_len), jnp.float32), pltpu.VMEM((tiles, tile_len, HD), jnp.float32)]
        + [pltpu.VMEM(shape, queries.dtype)] * 2
        + [pair, single, single, pair, each, pair, pair, pair, each, pair, pair],
        compiler_params=pltpu.CompilerParams(
            collective_id=0, has_side_effects=True, vmem_limit_bytes=51 * 1024 * 1024
        ),
    )(neighbours, queries.reshape(shape), keys.reshape(shape), values.reshape(shape))
    return out.reshape(tokens, width)


def solution(mesh):
    spec = P(("groups", "blk"), None)
    return jax.shard_map(
        functools.partial(on_device, mesh.shape["blk"]),
        mesh=mesh, in_specs=(spec,) * 4, out_specs=spec, check_vma=False,
    )
```

time: 124 us -> 121 us (0.976)
  Pallas kernels: 121 us -> 118 us
    pallas_call x1, Pallas kernels: 121 us -> 118 us  [on_device(): pl.pallas_call(functools.partial(kernel, count, heads), out_shape=jax.Sha...]
    unnamed x1 -> x3, local copies, waits for them, and re-layouts: 3.22 us -> 2.09 us
where the time goes in v1:
time: 121 us; the launch traced here: 120 us
  Pallas kernels  118 us (98%)
  local copies, waits for them, and re-layouts  2.09 us (2%)
    pallas_call x1, Pallas kernels, on_device(): pl.pallas_call(functools.partial(kernel, count, heads), out_shape=jax.Sha...  118 us

profile of v1, /device:TPU:15, one launch (start us, length us, event | category | flops | bytes accessed | tf_op | source)
XLA Modules:
  0.0 119.8 jit_solution(2163053799645692692)
XLA Ops:
  0.0 0.0 copy-start
  0.0 0.7 copy-done
  0.7 117.7 %shard_map.46 = bf16[2,384,1536]{2,1,0:T(8,128)(2,1)S(1)} custom-call(s32[2,7]{1,0:T(2,128)S(1)} %copy-done, bf16[2,384,1536]{2,1,0:T(8,128)(2,1)} %bitcast.5, bf16[2,384,1536]{2,1,0:T(8,128)(2,1)} %bitcast.6, bf16[2,384,1536]{2,1,0:T(8,128)(2,1)} %bitcast.7), custom_call_target="tpu_custom_call" | custom-call | tf_op jit(solution)/shard_map/pallas_call | solution.py:262
  118.4 1.4 %copy.6 = bf16[768,1536]{1,0:T(8,128)(2,1)} copy(bf16[768,1536]{1,0:T(8,128)(2,1)S(1)} %bitcast.4) | data formatting | bytes 4718592
Async XLA Ops:
  0.0 0.7 copy-start

commit v2 on v1

v2 whole, which is shorter than its diff:
```python
import functools
import math
from typing import Any, NamedTuple

import jax
import jax.numpy as jnp
from jax import lax
from jax.experimental import pallas as pl
from jax.experimental.pallas import tpu as pltpu
from jax.sharding import PartitionSpec as P

HD = 128
WINDOW = 5
ROWS = 128


class Chunk(NamedTuple):
    index: int
    which: int
    head: int
    first: int
    rows: int
    window: Any

    @property
    def pieces(self):
        return self.rows // ROWS


def send_order(heads):
    order = [(head, which) for head in range(heads - 2) for which in range(2)]
    return order + [(heads - 2, 0), (heads - 1, 0), (heads - 2, 1), (heads - 1, 1)]


def kernel(count, heads, neighbours, queries, keys, values, out, *scratch):
    windows = scratch[: 2 * heads + 1]
    (scores, tops, rounded, totals, sums, held_q, named, named_sem, local_sem, q_sem,
     y_send, y_recv, sib_send, sib_recv, z_send, z_recv, share_send, share_recv, wide_send, ready) = scratch[2 * heads + 1 :]
    sources = (keys, values)
    tiles, tile_len, _ = queries.shape
    slots = neighbours.shape[1]
    factor = math.log2(math.e) * HD ** -0.5

    chunks = []
    for index, (head, which) in enumerate(send_order(heads)):
        first = 0
        while first < tile_len:
            left = windows[len(chunks)].shape[1]
            chunks.append(Chunk(len(chunks), which, head, first, left, windows[len(chunks)]))
            first += left

    def chunk_of(head, which):
        return [c for c in chunks if (c.head, c.which) == (head, which)]

    me = lax.axis_index("blk")
    core = lax.rem(me, 2)
    side = lax.rem(me // 2, 2)
    quad = me // 4
    last = count // 4 - 1
    sibling = me + 1 - 2 * core
    partner = me + 2 - 4 * side
    ahead = me + 4 - 8 * side
    behind = me - 4 + 8 * side
    can_relay = jnp.where(side == 0, quad < last, quad > 0)
    gets_relay = jnp.where(side == 0, quad > 0, quad < last)
    shares_partner = core == side
    sends_wide = jnp.logical_and(side == 1, jnp.logical_and(jnp.logical_not(shares_partner), quad > 0))
    gets_wide = jnp.logical_and(side == 1, jnp.logical_and(shares_partner, quad < last))
    awaits_ready = jnp.logical_and(side == 0, quad < last)
    gives_ready = jnp.logical_and(side == 0, quad > 0)
    shares_relay = jnp.logical_and(jnp.logical_not(shares_partner), gets_relay)
    partner_at = 4 - 4 * side
    relay_at = 4 * side

    def strip(head):
        return pl.ds(head * HD, HD)

    def part(c, block, piece):
        at = pl.ds(block * tiles, tiles)
        return c.window.at[at] if piece is None else c.window.at[at, pl.ds(piece * ROWS, ROWS)]

    def from_source(c, piece):
        if piece is None:
            return sources[c.which].at[:, pl.ds(c.first, c.rows), strip(c.head)]
        return sources[c.which].at[:, pl.ds(c.first + piece * ROWS, ROWS), strip(c.head)]

    def remote(src, dst, send, recv, target):
        return pltpu.make_async_remote_copy(
            src_ref=src, dst_ref=dst, send_sem=send, recv_sem=recv,
            device_id={"blk": target}, device_id_type=pl.DeviceIdType.MESH,
        )

    def partner_copy(c, piece=None):
        return remote(from_source(c, piece), part(c, relay_at, piece), y_send.at[c.index],
                      y_recv.at[c.index, 0 if piece is None else piece], partner)

    def relay_copy(c, piece=None):
        return remote(part(c, partner_at, piece), part(c, relay_at, piece), z_send.at[c.index],
                      z_recv.at[c.index, 0 if piece is None else piece], ahead)

    def share_copy(c, piece=None):
        return remote(part(c, 4 - 4 * core, piece), part(c, 3 - 2 * core, piece),
                      share_send.at[c.index], share_recv.at[c.index], sibling)

    def wide_copy(c):
        return remote(part(c, partner_at, None), part(c, 3 - 2 * core, None), wide_send,
                      share_recv.at[c.index], ahead + 1 - 2 * core)

    def own(c, tile, block):
        if tile is None:
            return from_source(c, None), part(c, block, None)
        src = sources[c.which].at[tile, pl.ds(c.first, c.rows), strip(c.head)]
        return src, c.window.at[block * tiles + tile]

    def sibling_copy(c, tile=None):
        return remote(*own(c, tile, 1 + 2 * core), sib_send.at[c.index], sib_recv.at[c.index], sibling)

    def local_copy(c, tile=None):
        return pltpu.make_async_copy(*own(c, tile, 2), local_sem.at[c.index])

    def query_copy(head, tile=None):
        at = slice(None) if tile is None else tile
        return pltpu.make_async_copy(
            queries.at[at, :, strip(head)], held_q.at[at, :, strip(head)], q_sem.at[head])

    table_copy = pltpu.make_async_copy(neighbours, named, named_sem)

    def send(c, tile):
        partner_copy(c, tile).start()
        sibling_copy(c, tile).start()
        local_copy(c, tile).start()
        if c.which == 0:
            query_copy(c.head, tile).start()

    def send_rest(c):
        for piece in range(tiles, c.pieces):
            partner_copy(c, piece).start()

    def send_short(c):
        for piece in range(c.pieces):
            partner_copy(c, piece).start()
        for tile in range(tiles):
            sibling_copy(c, tile).start()
            local_copy(c, tile).start()

    def pass_on(c, piece):
        partner_copy(c, piece).wait_recv()

        @pl.when(can_relay)
        def _():
            relay_copy(c, piece).start()

        @pl.when(shares_partner)
        def _():
            share_copy(c, piece).start()

    def share_relay(c, piece):
        @pl.when(shares_relay)
        def _():
            relay_copy(c, piece).wait_recv()
            share_copy(c, piece).start()

    def gather(c):
        local_copy(c).wait()
        sibling_copy(c).wait_recv()

        took = jnp.logical_and(side == 0, shares_relay) if c.pieces == 1 else shares_relay

        @pl.when(jnp.logical_and(gets_relay, jnp.logical_not(took)))
        def _():
            for piece in range(c.pieces):
                relay_copy(c, piece).wait_recv()

        @pl.when(jnp.logical_or(jnp.logical_not(shares_partner), gets_relay))
        def _():
            share_copy(c).wait_recv()

    def drain(c):
        partner_copy(c).wait_send()
        sibling_copy(c).wait_send()

        @pl.when(can_relay)
        def _():
            relay_copy(c).wait_send()

        passed = jnp.logical_and(side == 0, shares_relay) if c.pieces == 1 else shares_relay

        @pl.when(jnp.logical_or(shares_partner, passed))
        def _():
            share_copy(c).wait_send()

    def place_of(tile, slot):
        entry = named[tile, slot]
        ok = entry >= 0
        place = jnp.where(ok, entry - (me - 2) * tiles, 2 * tiles + tile)
        return ok, jnp.clip(place, 0, WINDOW * tiles - 1)

    def score(head, tile, room):
        (c,) = chunk_of(head, 0)
        query = held_q[tile, :, strip(head)]
        peak = None
        for slot in range(slots):
            score = lax.dot_general(
                query, c.window[place_of(tile, slot)[1]], (((1,), (1,)), ((), ())),
                preferred_element_type=jnp.float32,
            )
            scores[room, slot] = score
            for lane in range(0, tile_len, HD):
                lanes = score[:, lane : lane + HD]
                peak = lanes if peak is None else jnp.maximum(peak, lanes)
        top = jnp.max(peak, axis=1, keepdims=True) * factor
        tops[room] = jnp.broadcast_to(top, tops.shape[1:])

    def weigh(room, slot, ok):
        offset = jnp.where(ok, tops[room, :, 0:1], jnp.inf)
        return jnp.exp2(scores[room, slot] * factor - offset)

    def mix(head, tile):
        (c,) = chunk_of(head, 1)
        total = jnp.zeros((tile_len, HD), jnp.float32)
        summed = jnp.zeros((tile_len, HD), jnp.float32)
        for slot in range(slots):
            ok, place = place_of(tile, slot)
            weights = weigh(tile, slot, ok)
            for lane in range(0, tile_len, HD):
                total += weights[:, lane : lane + HD]
            summed += jnp.dot(
                weights.astype(jnp.bfloat16), c.window[place], preferred_element_type=jnp.float32)
        out[tile, :, strip(head)] = (summed / jnp.sum(total, axis=1, keepdims=True)).astype(out.dtype)

    def settle(tile, room):
        total = jnp.zeros((tile_len, HD), jnp.float32)
        for slot in range(slots):
            ok, _ = place_of(tile, slot)
            weights = weigh(room, slot, ok)
            for lane in range(0, tile_len, HD):
                total += weights[:, lane : lane + HD]
            rounded[tile, slot] = weights.astype(jnp.bfloat16)
        totals[tile] = jnp.broadcast_to(jnp.sum(total, axis=1, keepdims=True), totals.shape[1:])

    def collect(c, tile):
        summed = jnp.zeros((tile_len, HD), jnp.float32)
        for slot in range(slots):
            _, place = place_of(tile, slot)
            summed += jnp.dot(
                rounded[tile, slot, :, c.first : c.first + c.rows], c.window[place],
                preferred_element_type=jnp.float32)
        return summed

    barrier = pltpu.get_barrier_semaphore()

    def greet(target):
        pl.semaphore_signal(barrier, inc=1, device_id={"blk": target}, device_id_type=pl.DeviceIdType.MESH)

    greet(partner)
    greet(sibling)

    @pl.when(quad < last)
    def _():
        greet(me + 4)

    @pl.when(gets_wide)
    def _():
        greet(me + 5 - 2 * core)

    pl.semaphore_wait(barrier, 2 + (quad > 0).astype(jnp.int32) + sends_wide.astype(jnp.int32))

    whole = [c for c in chunks if c.rows == tile_len]
    first_part, last_part = chunks[len(whole) :]
    final = heads - 1
    (final_keys,) = chunk_of(final, 0)
    (late_values,) = chunk_of(final - 1, 1)

    for c in chunks[:2]:
        for tile in range(tiles):
            send(c, tile)
        send_rest(c)
        if c.index == 0:
            table_copy.start()
    ordered = [(head, which) for head in range(heads - 2) for which in range(2)]

    @pl.when(gives_ready)
    def _():
        pl.semaphore_signal(ready, inc=1, device_id={"blk": behind}, device_id_type=pl.DeviceIdType.MESH)

    @pl.when(awaits_ready)
    def _():
        pl.semaphore_wait(ready, 1)

    for c in chunks[:-3]:
        task = ordered[c.index - 2] if c.index >= 2 else None

        pass_on(c, 0)
        if c.index > 0:
            share_relay(chunks[c.index - 1], 0)

        @pl.loop(0, tiles)
        def _(tile):
            pass_on(c, tile + 1)
            if c.index > 0:
                share_relay(chunks[c.index - 1], tile + 1)
            send(chunks[c.index + 2], tile)
            if task:
                @pl.when(tile == 0)
                def _():
                    if c.index == 2:
                        table_copy.wait()
                    if task[1] == 0:
                        query_copy(task[0]).wait()
                    gather(*chunk_of(*task))

                if task[1] == 0:
                    score(task[0], tile, tile)
                else:
                    mix(task[0], tile)

        send_rest(chunks[c.index + 2])
        if c.index + 2 == first_part.index:
            send_short(last_part)
        if c.index >= 2:
            drain(chunks[c.index - 2])

    pass_on(late_values, 0)
    share_relay(final_keys, 0)

    @pl.loop(0, tiles)
    def _(tile):
        pass_on(late_values, tile + 1)
        share_relay(final_keys, tile + 1)

        @pl.when(tile == 0)
        def _():
            query_copy(final - 1).wait()
            gather(*chunk_of(final - 1, 0))

        score(final - 1, tile, tile)

    drain(chunks[late_values.index - 2])
    pass_on(first_part, 0)
    share_relay(late_values, 0)
    query_copy(final).wait()
    gather(final_keys)

    @pl.loop(0, tiles)
    def _(tile):
        score(final, tile, tiles)

        @pl.when(tile == 0)
        def _():
            pass_on(first_part, 1)
            share_relay(late_values, 1)

        settle(tile, tiles)

        @pl.when(tile == 0)
        def _():
            pass_on(last_part, 0)

            @pl.when(sends_wide)
            def _():
                wide_copy(last_part).start()

            share_relay(late_values, 2)

    share_relay(first_part, 0)
    gather(late_values)

    @pl.loop(0, tiles)
    def _(tile):
        mix(final - 1, tile)

        @pl.when(tile == 0)
        def _():
            share_relay(first_part, 1)

        @pl.when(jnp.logical_and(tile == 1, side == 0))
        def _():
            share_relay(last_part, 0)

    drain(chunks[late_values.index - 1])
    drain(late_values)
    gather(first_part)

    @pl.loop(0, tiles)
    def _(tile):
        sums[tile] = collect(first_part, tile)

    gather(last_part)

    @pl.loop(0, tiles)
    def _(tile):
        summed = sums[tile] + collect(last_part, tile)
        out[tile, :, strip(final)] = (summed / totals[tile]).astype(out.dtype)

    drain(first_part)
    drain(last_part)

    @pl.when(sends_wide)
    def _():
        wide_copy(last_part).wait_send()


def on_device(count, queries, keys, values, neighbours):
    tokens, width = queries.shape
    tiles, slots = neighbours.shape
    tile_len = tokens // tiles
    heads = width // HD
    shape = (tiles, tile_len, width)
    lengths = [tile_len] * (2 * heads - 1) + [tile_len - ROWS, ROWS]
    windows = [pltpu.VMEM((WINDOW * tiles, length, HD), queries.dtype) for length in lengths]
    column = pltpu.VMEM((tiles, tile_len, HD), jnp.float32)
    per_chunk = pltpu.SemaphoreType.DMA((len(lengths),))
    per_piece = pltpu.SemaphoreType.DMA((len(lengths), tile_len // ROWS))
    hbm = pl.BlockSpec(memory_space=pl.ANY)
    neighbours = pltpu.with_memory_space_constraint(neighbours, pltpu.HBM)
    out = pl.pallas_call(
        functools.partial(kernel, count, heads),
        out_shape=jax.ShapeDtypeStruct(shape, queries.dtype),
        in_specs=[hbm, hbm, hbm, hbm],
        out_specs=pl.BlockSpec(memory_space=pltpu.VMEM),
        scratch_shapes=windows
        + [
            pltpu.VMEM((tiles + 1, slots, tile_len, tile_len), jnp.float32),
            pltpu.VMEM((tiles + 1, tile_len, HD), jnp.float32),
            pltpu.VMEM((tiles, slots, tile_len, tile_len), jnp.bfloat16),
            column,
            column,
            pltpu.VMEM(shape, queries.dtype),
            pltpu.SMEM((tiles, slots), jnp.int32),
            pltpu.SemaphoreType.DMA,
            per_chunk,
            pltpu.SemaphoreType.DMA((heads,)),
        ]
        + [per_chunk, per_piece, per_chunk, per_chunk, per_chunk, per_piece, per_chunk, per_chunk]
        + [pltpu.SemaphoreType.DMA, pltpu.SemaphoreType.REGULAR],
        compiler_params=pltpu.CompilerParams(
            collective_id=0, has_side_effects=True, vmem_limit_bytes=51 * 1024 * 1024
        ),
    )(neighbours, queries.reshape(shape), keys.reshape(shape), values.reshape(shape))
    return out.reshape(tokens, width)


def solution(mesh):
    spec = P(("groups", "blk"), None)
    return jax.shard_map(
        functools.partial(on_device, mesh.shape["blk"]),
        mesh=mesh, in_specs=(spec,) * 4, out_specs=spec, check_vma=False,
    )
```

time: 121 us -> 116 us (0.959)
  Pallas kernels: 118 us -> 114 us
    pallas_call x1, Pallas kernels: 118 us -> 114 us  [on_device(): pl.pallas_call(functools.partial(kernel, count, heads), out_shape=jax.Sha...]
where the time goes in v2:
time: 116 us; the launch traced here: 115 us
  Pallas kernels  114 us (98%)
  local copies, waits for them, and re-layouts  1.41 us (1%)
    pallas_call x1, Pallas kernels, on_device(): pl.pallas_call(functools.partial(kernel, count, heads), out_shape=jax.Sha...  114 us

profile of v2, /device:TPU:15, one launch (start us, length us, event | category | flops | bytes accessed | tf_op | source)
XLA Modules:
  0.0 115.5 jit_solution(7188963780084912566)
XLA Ops:
  0.0 114.0 %shard_map.46 = bf16[2,384,1536]{2,1,0:T(8,128)(2,1)S(1)} custom-call(s32[2,7]{1,0:T(2,128)} %neighbours.1, bf16[2,384,1536]{2,1,0:T(8,128)(2,1)} %bitcast.5, bf16[2,384,1536]{2,1,0:T(8,128)(2,1)} %bitcast.6, bf16[2,384,1536]{2,1,0:T(8,128)(2,1)} %bitcast.7), custom_call_target="tpu_custom_call" | custom-call | tf_op jit(solution)/shard_map/pallas_call | solution.py:416
  114.1 1.4 %copy.6 = bf16[768,1536]{1,0:T(8,128)(2,1)} copy(bf16[768,1536]{1,0:T(8,128)(2,1)S(1)} %bitcast.4) | data formatting | bytes 4718592

commit v3 on v2

--- a/solution.py
+++ b/solution.py
@@ -12,6 +12,10 @@
 HD = 128
 WINDOW = 5
 ROWS = 128
+SENDS = 6
+LANDS = 10
+SHARES = 8
+QUERIES = 4
 
 
 class Chunk(NamedTuple):
@@ -29,14 +33,15 @@
 
 def send_order(heads):
     order = [(head, which) for head in range(heads - 2) for which in range(2)]
-    return order + [(heads - 2, 0), (heads - 1, 0), (heads - 2, 1), (heads - 1, 1)]
+    return order + [(heads - 1, 0), (heads - 2, 0), (heads - 2, 1), (heads - 1, 1)]
 
 
 def kernel(count, heads, neighbours, queries, keys, values, out, *scratch):
     windows = scratch[: 2 * heads + 1]
-    (scores, tops, rounded, totals, sums, held_q, named, named_sem, local_sem, q_sem,
+    (scores, tops, rounded_first, rounded_last, gathered_first, gathered_last, totals, sums, held_q, named, named_sem, local_sem, q_sem,
      y_send, y_recv, sib_send, sib_recv, z_send, z_recv, share_send, share_recv, wide_send, ready) = scratch[2 * heads + 1 :]
     sources = (keys, values)
+    rounded, gathered = (rounded_first, rounded_last), (gathered_first, gathered_last)
     tiles, tile_len, _ = queries.shape
     slots = neighbours.shape[1]
     factor = math.log2(math.e) * HD ** -0.5
@@ -91,20 +96,23 @@
         )
 
     def partner_copy(c, piece=None):
-        return remote(from_source(c, piece), part(c, relay_at, piece), y_send.at[c.index],
-                      y_recv.at[c.index, 0 if piece is None else piece], partner)
+        return remote(from_source(c, piece), part(c, relay_at, piece), y_send.at[c.index % SENDS],
+                      y_recv.at[c.index % SENDS, 0 if piece is None else piece], partner)
 
     def relay_copy(c, piece=None):
-        return remote(part(c, partner_at, piece), part(c, relay_at, piece), z_send.at[c.index],
-                      z_recv.at[c.index, 0 if piece is None else piece], ahead)
+        return remote(part(c, partner_at, piece), part(c, relay_at, piece), z_send.at[c.index % SENDS],
+                      z_recv.at[c.index % LANDS, 0 if piece is None else piece], ahead)
+
+    def share_slot(c):
+        return SHARES if c.pieces == 1 else c.index % SHARES
 
     def share_copy(c, piece=None):
         return remote(part(c, 4 - 4 * core, piece), part(c, 3 - 2 * core, piece),
-                      share_send.at[c.index], share_recv.at[c.index], sibling)
+                      share_send.at[c.index % SENDS], share_recv.at[share_slot(c)], sibling)
 
     def wide_copy(c):
         return remote(part(c, partner_at, None), part(c, 3 - 2 * core, None), wide_send,
-                      share_recv.at[c.index], ahead + 1 - 2 * core)
+                      share_recv.at[share_slot(c)], ahead + 1 - 2 * core)
 
     def own(c, tile, block):
         if tile is None:
@@ -113,15 +121,15 @@
         return src, c.window.at[block * tiles + tile]
 
     def sibling_copy(c, tile=None):
-        return remote(*own(c, tile, 1 + 2 * core), sib_send.at[c.index], sib_recv.at[c.index], sibling)
+        return remote(*own(c, tile, 1 + 2 * core), sib_send.at[c.index % SENDS], sib_recv.at[c.index % LANDS], sibling)
 
     def local_copy(c, tile=None):
-        return pltpu.make_async_copy(*own(c, tile, 2), local_sem.at[c.index])
+        return pltpu.make_async_copy(*own(c, tile, 2), local_sem.at[c.index % SENDS])
 
     def query_copy(head, tile=None):
         at = slice(None) if tile is None else tile
         return pltpu.make_async_copy(
-            queries.at[at, :, strip(head)], held_q.at[at, :, strip(head)], q_sem.at[head])
+            queries.at[at, :, strip(head)], held_q.at[at, :, strip(head)], q_sem.at[head % QUERIES])
 
     table_copy = pltpu.make_async_copy(neighbours, named, named_sem)
 
@@ -235,17 +243,16 @@
             weights = weigh(room, slot, ok)
             for lane in range(0, tile_len, HD):
                 total += weights[:, lane : lane + HD]
-            rounded[tile, slot] = weights.astype(jnp.bfloat16)
+            weights = weights.astype(jnp.bfloat16)
+            for ref, c in zip(rounded, chunks[-2:]):
+                ref[tile, :, slot * c.rows : (slot + 1) * c.rows] = weights[:, c.first : c.first + c.rows]
         totals[tile] = jnp.broadcast_to(jnp.sum(total, axis=1, keepdims=True), totals.shape[1:])
 
-    def collect(c, tile):
-        summed = jnp.zeros((tile_len, HD), jnp.float32)
+    def collect(part, tile):
+        c, held = chunks[part - 2], gathered[part]
         for slot in range(slots):
-            _, place = place_of(tile, slot)
-            summed += jnp.dot(
-                rounded[tile, slot, :, c.first : c.first + c.rows], c.window[place],
-                preferred_element_type=jnp.float32)
-        return summed
+            held[slot * c.rows : (slot + 1) * c.rows] = c.window[place_of(tile, slot)[1]]
+        return jnp.dot(rounded[part][tile], held[...], preferred_element_type=jnp.float32)
 
     barrier = pltpu.get_barrier_semaphore()
 
@@ -269,14 +276,19 @@
     first_part, last_part = chunks[len(whole) :]
     final = heads - 1
     (final_keys,) = chunk_of(final, 0)
+    (late_keys,) = chunk_of(final - 1, 0)
     (late_values,) = chunk_of(final - 1, 1)
 
-    for c in chunks[:2]:
-        for tile in range(tiles):
-            send(c, tile)
-        send_rest(c)
-        if c.index == 0:
-            table_copy.start()
+    for piece in range(chunks[0].pieces):
+        partner_copy(chunks[0], piece).start()
+    for tile in range(tiles):
+        sibling_copy(chunks[0], tile).start()
+        local_copy(chunks[0], tile).start()
+        query_copy(0, tile).start()
+    table_copy.start()
+    for tile in range(tiles):
+        send(chunks[1], tile)
+    send_rest(chunks[1])
     ordered = [(head, which) for head in range(heads - 2) for which in range(2)]
 
     @pl.when(gives_ready)
@@ -321,23 +333,7 @@
             drain(chunks[c.index - 2])
 
     pass_on(late_values, 0)
-    share_relay(final_keys, 0)
-
-    @pl.loop(0, tiles)
-    def _(tile):
-        pass_on(late_values, tile + 1)
-        share_relay(final_keys, tile + 1)
-
-        @pl.when(tile == 0)
-        def _():
-            query_copy(final - 1).wait()
-            gather(*chunk_of(final - 1, 0))
-
-        score(final - 1, tile, tile)
-
-    drain(chunks[late_values.index - 2])
-    pass_on(first_part, 0)
-    share_relay(late_values, 0)
+    share_relay(late_keys, 0)
     query_copy(final).wait()
     gather(final_keys)
 
@@ -347,10 +343,30 @@
 
         @pl.when(tile == 0)
         def _():
-            pass_on(first_part, 1)
-            share_relay(late_values, 1)
+            pass_on(late_values, 1)
+            share_relay(late_keys, 1)
+
+        @pl.when(tile == 1)
+        def _():
+            pass_on(first_part, 0)
+            share_relay(late_values, 0)
 
         settle(tile, tiles)
+
+        @pl.when(tile == 0)
+        def _():
+            pass_on(late_values, 2)
+            share_relay(late_keys, 2)
+
+    drain(final_keys)
+    query_copy(final - 1).wait()
+    gather(late_keys)
+    pass_on(first_part, 1)
+    share_relay(late_values, 1)
+
+    @pl.loop(0, tiles)
+    def _(tile):
+        score(final - 1, tile, tile)
 
         @pl.when(tile == 0)
         def _():
@@ -377,19 +393,19 @@
         def _():
             share_relay(last_part, 0)
 
-    drain(chunks[late_values.index - 1])
+    drain(late_keys)
     drain(late_values)
     gather(first_part)
 
     @pl.loop(0, tiles)
     def _(tile):
-        sums[tile] = collect(first_part, tile)
+        sums[tile] = collect(0, tile)
 
     gather(last_part)
 
     @pl.loop(0, tiles)
     def _(tile):
-        summed = sums[tile] + collect(last_part, tile)
+        summed = sums[tile] + collect(1, tile)
         out[tile, :, strip(final)] = (summed / totals[tile]).astype(out.dtype)
 
     drain(first_part)
@@ -409,8 +425,8 @@
     lengths = [tile_len] * (2 * heads - 1) + [tile_len - ROWS, ROWS]
     windows = [pltpu.VMEM((WINDOW * tiles, length, HD), queries.dtype) for length in lengths]
     column = pltpu.VMEM((tiles, tile_len, HD), jnp.float32)
-    per_chunk = pltpu.SemaphoreType.DMA((len(lengths),))
-    per_piece = pltpu.SemaphoreType.DMA((len(lengths), tile_len // ROWS))
+    pieces = tile_len // ROWS
+    sends = pltpu.SemaphoreType.DMA((SENDS,))
     hbm = pl.BlockSpec(memory_space=pl.ANY)
     neighbours = pltpu.with_memory_space_constraint(neighbours, pltpu.HBM)
     out = pl.pallas_call(
@@ -422,16 +438,20 @@
         + [
             pltpu.VMEM((tiles + 1, slots, tile_len, tile_len), jnp.float32),
             pltpu.VMEM((tiles + 1, tile_len, HD), jnp.float32),
-            pltpu.VMEM((tiles, slots, tile_len, tile_len), jnp.bfloat16),
+            pltpu.VMEM((tiles, tile_len, slots * lengths[-2]), jnp.bfloat16),
+            pltpu.VMEM((tiles, tile_len, slots * lengths[-1]), jnp.bfloat16),
+            pltpu.VMEM((slots * lengths[-2], HD), queries.dtype),
+            pltpu.VMEM((slots * lengths[-1], HD), queries.dtype),
             column,
             column,
             pltpu.VMEM(shape, queries.dtype),
             pltpu.SMEM((tiles, slots), jnp.int32),
             pltpu.SemaphoreType.DMA,
-            per_chunk,
-            pltpu.SemaphoreType.DMA((heads,)),
+            sends,
+            pltpu.SemaphoreType.DMA((QUERIES,)),
         ]
-        + [per_chunk, per_piece, per_chunk, per_chunk, per_chunk, per_piece, per_chunk, per_chunk]
+        + [sends, pltpu.SemaphoreType.DMA((SENDS, pieces)), sends, pltpu.SemaphoreType.DMA((LANDS,))]
+        + [sends, pltpu.SemaphoreType.DMA((LANDS, pieces)), sends, pltpu.SemaphoreType.DMA((SHARES + 1,))]
         + [pltpu.SemaphoreType.DMA, pltpu.SemaphoreType.REGULAR],
         compiler_params=pltpu.CompilerParams(
             collective_id=0, has_side_effects=True, vmem_limit_bytes=51 * 1024 * 1024

time: 116 us -> 114 us (0.983)
  Pallas kernels: 114 us -> 112 us
    pallas_call x1, Pallas kernels: 114 us -> 112 us  [on_device(): pl.pallas_call(functools.partial(kernel, count, heads), out_shape=jax.Sha...]
where the time goes in v3:
time: 114 us
  Pallas kernels  112 us (98%)
  local copies, waits for them, and re-layouts  1.41 us (1%)
    pallas_call x1, Pallas kernels, on_device(): pl.pallas_call(functools.partial(kernel, count, heads), out_shape=jax.Sha...  112 us

profile of v3, /device:TPU:15, one launch (start us, length us, event | category | flops | bytes accessed | tf_op | source)
XLA Modules:
  0.0 113.6 jit_solution(15585433138661730782)
XLA Ops:
  0.0 112.2 %shard_map.46 = bf16[2,384,1536]{2,1,0:T(8,128)(2,1)S(1)} custom-call(s32[2,7]{1,0:T(2,128)} %neighbours.1, bf16[2,384,1536]{2,1,0:T(8,128)(2,1)} %bitcast.5, bf16[2,384,1536]{2,1,0:T(8,128)(2,1)} %bitcast.6, bf16[2,384,1536]{2,1,0:T(8,128)(2,1)} %bitcast.7), custom_call_target="tpu_custom_call" | custom-call | tf_op jit(solution)/shard_map/pallas_call | solution.py:432
  112.2 1.4 %copy.6 = bf16[768,1536]{1,0:T(8,128)(2,1)} copy(bf16[768,1536]{1,0:T(8,128)(2,1)S(1)} %bitcast.4) | data formatting | bytes 4718592

commit v4 on v3

--- a/solution.py
+++ b/solution.py
@@ -12,9 +12,10 @@
 HD = 128
 WINDOW = 5
 ROWS = 128
-SENDS = 6
-LANDS = 10
-SHARES = 8
+SENDS = 5
+LANDS = 9
+SHARES = 7
+RELAYS = 4
 QUERIES = 4
 
 
@@ -69,8 +70,8 @@
     can_relay = jnp.where(side == 0, quad < last, quad > 0)
     gets_relay = jnp.where(side == 0, quad > 0, quad < last)
     shares_partner = core == side
-    sends_wide = jnp.logical_and(side == 1, jnp.logical_and(jnp.logical_not(shares_partner), quad > 0))
-    gets_wide = jnp.logical_and(side == 1, jnp.logical_and(shares_partner, quad < last))
+    sends_wide = count < 0
+    gets_wide = count < 0
     awaits_ready = jnp.logical_and(side == 0, quad < last)
     gives_ready = jnp.logical_and(side == 0, quad > 0)
     shares_relay = jnp.logical_and(jnp.logical_not(shares_partner), gets_relay)
@@ -100,7 +101,7 @@
                       y_recv.at[c.index % SENDS, 0 if piece is None else piece], partner)
 
     def relay_copy(c, piece=None):
-        return remote(part(c, partner_at, piece), part(c, relay_at, piece), z_send.at[c.index % SENDS],
+        return remote(part(c, partner_at, piece), part(c, relay_at, piece), z_send.at[c.index % RELAYS],
                       z_recv.at[c.index % LANDS, 0 if piece is None else piece], ahead)
 
     def share_slot(c):
@@ -108,7 +109,7 @@
 
     def share_copy(c, piece=None):
         return remote(part(c, 4 - 4 * core, piece), part(c, 3 - 2 * core, piece),
-                      share_send.at[c.index % SENDS], share_recv.at[share_slot(c)], sibling)
+                      share_send.at[c.index % RELAYS], share_recv.at[share_slot(c)], sibling)
 
     def wide_copy(c):
         return remote(part(c, partner_at, None), part(c, 3 - 2 * core, None), wide_send,
@@ -172,7 +173,7 @@
         local_copy(c).wait()
         sibling_copy(c).wait_recv()
 
-        took = jnp.logical_and(side == 0, shares_relay) if c.pieces == 1 else shares_relay
+        took = shares_relay
 
         @pl.when(jnp.logical_and(gets_relay, jnp.logical_not(took)))
         def _():
@@ -191,7 +192,7 @@
         def _():
             relay_copy(c).wait_send()
 
-        passed = jnp.logical_and(side == 0, shares_relay) if c.pieces == 1 else shares_relay
+        passed = shares_relay
 
         @pl.when(jnp.logical_or(shares_partner, passed))
         def _():
@@ -266,11 +267,7 @@
     def _():
         greet(me + 4)
 
-    @pl.when(gets_wide)
-    def _():
-        greet(me + 5 - 2 * core)
-
-    pl.semaphore_wait(barrier, 2 + (quad > 0).astype(jnp.int32) + sends_wide.astype(jnp.int32))
+    pl.semaphore_wait(barrier, 2 + (quad > 0).astype(jnp.int32) )
 
     whole = [c for c in chunks if c.rows == tile_len]
     first_part, last_part = chunks[len(whole) :]
@@ -327,10 +324,10 @@
                     mix(task[0], tile)
 
         send_rest(chunks[c.index + 2])
+        if c.index >= 2:
+            drain(chunks[c.index - 2])
         if c.index + 2 == first_part.index:
             send_short(last_part)
-        if c.index >= 2:
-            drain(chunks[c.index - 2])
 
     pass_on(late_values, 0)
     share_relay(late_keys, 0)
@@ -370,13 +367,8 @@
 
         @pl.when(tile == 0)
         def _():
+            share_relay(late_values, 2)
             pass_on(last_part, 0)
-
-            @pl.when(sends_wide)
-            def _():
-                wide_copy(last_part).start()
-
-            share_relay(late_values, 2)
 
     share_relay(first_part, 0)
     gather(late_values)
@@ -389,7 +381,7 @@
         def _():
             share_relay(first_part, 1)
 
-        @pl.when(jnp.logical_and(tile == 1, side == 0))
+        @pl.when(tile == 1)
         def _():
             share_relay(last_part, 0)
 
@@ -410,10 +402,6 @@
 
     drain(first_part)
     drain(last_part)
-
-    @pl.when(sends_wide)
-    def _():
-        wide_copy(last_part).wait_send()
 
 
 def on_device(count, queries, keys, values, neighbours):
@@ -427,6 +415,7 @@
     column = pltpu.VMEM((tiles, tile_len, HD), jnp.float32)
     pieces = tile_len // ROWS
     sends = pltpu.SemaphoreType.DMA((SENDS,))
+    relays = pltpu.SemaphoreType.DMA((RELAYS,))
     hbm = pl.BlockSpec(memory_space=pl.ANY)
     neighbours = pltpu.with_memory_space_constraint(neighbours, pltpu.HBM)
     out = pl.pallas_call(
@@ -451,7 +440,7 @@
             pltpu.SemaphoreType.DMA((QUERIES,)),
         ]
         + [sends, pltpu.SemaphoreType.DMA((SENDS, pieces)), sends, pltpu.SemaphoreType.DMA((LANDS,))]
-        + [sends, pltpu.SemaphoreType.DMA((LANDS, pieces)), sends, pltpu.SemaphoreType.DMA((SHARES + 1,))]
+        + [relays, pltpu.SemaphoreType.DMA((LANDS, pieces)), relays, pltpu.SemaphoreType.DMA((SHARES + 1,))]
         + [pltpu.SemaphoreType.DMA, pltpu.SemaphoreType.REGULAR],
         compiler_params=pltpu.CompilerParams(
             collective_id=0, has_side_effects=True, vmem_limit_bytes=51 * 1024 * 1024

time: 114 us -> 114 us (level)
  no operation moved by 1% of the time
where the time goes in v4:
time: 114 us
  Pallas kernels  112 us (98%)
  local copies, waits for them, and re-layouts  1.41 us (1%)
    pallas_call x1, Pallas kernels, on_device(): pl.pallas_call(functools.partial(kernel, count, heads), out_shape=jax.Sha...  112 us

profile of v4, /device:TPU:15, one launch (start us, length us, event | category | flops | bytes accessed | tf_op | source)
XLA Modules:
  0.0 113.6 jit_solution(15050664745619630723)
XLA Ops:
  0.0 112.2 %shard_map.46 = bf16[2,384,1536]{2,1,0:T(8,128)(2,1)S(1)} custom-call(s32[2,7]{1,0:T(2,128)} %neighbours.1, bf16[2,384,1536]{2,1,0:T(8,128)(2,1)} %bitcast.5, bf16[2,384,1536]{2,1,0:T(8,128)(2,1)} %bitcast.6, bf16[2,384,1536]{2,1,0:T(8,128)(2,1)} %bitcast.7), custom_call_target="tpu_custom_call" | custom-call | tf_op jit(solution)/shard_map/pallas_call | solution.py:421
  112.2 1.4 %copy.6 = bf16[768,1536]{1,0:T(8,128)(2,1)} copy(bf16[768,1536]{1,0:T(8,128)(2,1)S(1)} %bitcast.4) | data formatting | bytes 4718592
